TPU v7x, 32 devices: a whole 2x2x4 slice. The times are simulated.
32 devices in a mesh: pair: 4 (over y, x), mat: 8 (over z, core).
Axes of the slice: x: 2, y: 2, z: 4, core: 2. Of those that a mesh axis runs over, the one named last changes fastest.
Arguments:
- operators: bfloat16 [16, 2048, 2048], P('pair', 'mat'), may hold values from -6 to 6
- left_rot: bfloat16 [2048, 2048], P('mat'), may hold values from -0.125 to 0.125
- right_rot: bfloat16 [2048, 2048], P('mat'), may hold values from -0.125 to 0.125
- integrals: float32 [1024, 1024], replicated, may hold values from -1.5 to 1.5
- pair_index: int32 [16], replicated, may hold values from 0 to 1023
- target_index: int32 [16], replicated, may hold values from 0 to 1023
Outputs:
- complement: bfloat16 [16, 2048, 2048], P('pair', None, 'mat')
All inputs are finite; a program needn't handle non-finite values.
Results may differ from a plain program's by a relative error of at most 0.0063.
Values may be sent and summed in bfloat16 or wider, within the bound.
A program may use at most 192 MiB of HBM per device.

v0:
```python
import jax
import jax.numpy as jnp
from jax import lax
from jax.sharding import PartitionSpec as P


def selector(indices, count):
    return (indices[:, None] == jnp.arange(count, dtype=jnp.int32)[None, :]).astype(jnp.float32)


def shards(operators, left_rot, right_rot, integrals, pair_index, target_index):
    half_sum = jnp.einsum(
        "krj,jm->krm",
        operators,
        lax.all_gather(right_rot, "mat", axis=0, tiled=True),
        preferred_element_type=jnp.float32,
    )
    half_rot = half_sum.astype(jnp.bfloat16)
    columns = lax.all_to_all(half_rot, "mat", split_axis=2, concat_axis=1, tiled=True)
    rot_sum = jnp.einsum(
        "rm,krc->kmc",
        lax.all_gather(left_rot, "mat", axis=0, tiled=True),
        columns,
        preferred_element_type=jnp.float32,
    )
    rotated = rot_sum.astype(jnp.bfloat16)
    npairs = integrals.shape[0]
    ntgt = target_index.shape[0]
    tdev = ntgt // lax.axis_size("pair")
    owned = lax.dynamic_slice_in_dim(target_index, lax.axis_index("pair") * tdev, tdev, 0)
    rowsel = jnp.dot(selector(owned, npairs), integrals, precision=lax.Precision.HIGHEST)
    coupling = jnp.dot(
        rowsel, selector(pair_index, npairs).T, precision=lax.Precision.HIGHEST
    ).astype(jnp.bfloat16)
    summed = jnp.einsum(
        "tk,kmc->tmc",
        coupling,
        lax.all_gather(rotated, "pair", axis=0, tiled=True),
        preferred_element_type=jnp.float32,
    )
    return summed.astype(jnp.bfloat16)


def solution(mesh):
    in_specs = (P("pair", "mat", None), P("mat", None), P("mat", None), P(), P(), P())
    out_specs = P("pair", None, "mat")
    return jax.shard_map(shards, mesh=mesh, in_specs=in_specs, out_specs=out_specs, check_vma=False)
```

profile of v0, /device:TPU:0, one launch (start us, length us, event | category | flops | bytes accessed | tf_op | source)
XLA Modules:
  0.0 477.3 jit_solution(13996536382218150171)
XLA Ops:
  6.5 0.0 all-gather.4.cloned.1.call-start
  6.5 0.7 all-gather.4.cloned.1.call-update
  7.3 0.0 all-gather.6.cloned.1.call-start
  7.3 0.7 all-gather.6.cloned.1.call-update
  8.0 0.0 all-gather.8.cloned.1.call-start
  8.1 85.7 %all-gather.4.cloned.1.call-done = bf16[2048,2048]{1,0:T(8,128)(2,1)} async-done(((bf16[256,2048]{1,0:T(8,128)(2,1)}), bf16[2048,2048]{1,0:T(8,128)(2,1)}) %all-gather.4.cloned.1.call-update) | async-done | bytes 8388624 | tf_op jit(solution)/shard_map/all_gather | solution.py:15
  93.7 13.8 %fusion.9 = bf16[4,256,2048]{2,1,0:T(8,128)(2,1)} fusion(bf16[4,256,2048]{2,1,0:T(8,128)(2,1)} %param.6, bf16[2048,2048]{1,0:T(8,128)(2,1)} %all-gather.4.cloned.1.call-done), kind=kOutput, calls=%fused_computation.8 | convolution fusion | flops 8592031744 | bytes 16777216 | tf_op jit(solution)/shard_map/krj,jm->krm/dot_general | solution.py:12
  107.5 7.5 %copy.15 = bf16[4,256,2048]{1,0,2:T(4,128)(2,1)} copy(bf16[4,256,2048]{2,1,0:T(8,128)(2,1)} %fusion.9) | data formatting | bytes 8388608 | tf_op jit(solution)/shard_map/convert_element_type | solution.py:18
  115.0 148.8 %all_to_all.18 = bf16[4,256,2048]{1,0,2:T(4,128)(2,1)S(1)} all-to-all(bf16[4,256,2048]{1,0,2:T(4,128)(2,1)} %copy.15), channel_id=1, replica_groups=mesh['pair'=4,'mat'=8] {'mat'}, dimensions={2} | all-to-all | bytes 8388608 | tf_op jit(solution)/shard_map/all_to_all | solution.py:19
  263.8 2.6 copy.16
  266.3 6.3 %copy.17 = bf16[4,8,256,256]{3,2,1,0:T(8,128)(2,1)} copy(bf16[4,8,256,256]{2,3,1,0:T(8,128)(2,1)} %bitcast.23) | data formatting | bytes 8388608 | tf_op jit(solution)/shard_map/all_to_all | solution.py:19
  272.6 0.0 all-gather.6.cloned.1.call-done
  272.6 13.9 %convert_bitcast_fusion = bf16[4,2048,256]{1,2,0:T(8,128)(2,1)} fusion(bf16[4,2048,256]{2,1,0:T(8,128)(2,1)} %bitcast.24, bf16[2048,2048]{1,0:T(8,128)(2,1)} %all-gather.6.cloned.1.call-done), kind=kOutput, calls=%fused_computation.7 | convolution fusion | flops 8592031744 | bytes 16777216 | tf_op jit(solution)/shard_map/rm,krc->kmc/dot_general | solution.py:20
  286.5 6.2 %copy.19 = bf16[4,2048,256]{2,1,0:T(8,128)(2,1)} copy(bf16[4,2048,256]{1,2,0:T(8,128)(2,1)} %convert_bitcast_fusion) | data formatting | bytes 8388608 | tf_op jit(solution)/shard_map/convert_element_type | solution.py:26
  292.7 0.0 copy-start
  292.7 0.0 copy-start.1
  292.7 0.0 all-gather.8.cloned.1.call-update
  292.8 0.6 copy-done
  293.4 0.1 dynamic_slice.3
  293.5 3.6 fusion.16
  297.1 0.0 copy-done.1
  297.1 0.2 fusion.14
  297.3 151.3 %all-gather.8.cloned.1.call-done = bf16[16,2048,256]{2,1,0:T(8,128)(2,1)} async-done(((bf16[4,2048,256]{2,1,0:T(8,128)(2,1)}), bf16[16,2048,256]{2,1,0:T(8,128)(2,1)}) %all-gather.8.cloned.1.call-update) | async-done | bytes 16777232 | tf_op jit(solution)/shard_map/all_gather | solution.py:38
  448.6 17.5 %fusion.6 = bf16[4,2048,256]{2,0,1:T(4,128)(2,1)} fusion(bf16[4,16,1]{1,0,2:T(4,128)(2,1)S(1)} %fusion.14, bf16[16,2048,256]{2,1,0:T(8,128)(2,1)} %all-gather.8.cloned.1.call-done), kind=kOutput, calls=%fused_computation.6 | convolution fusion | flops 69206016 | bytes 20971648 | tf_op jit(solution)/shard_map/tk,kmc->tmc/dot_general | solution.py:35
  466.1 4.7 copy.21
Async XLA Ops:
  6.5 87.2 %all-gather.4.cloned.1.call-start = ((), (), s32[]{:S(2)}) async-start(), calls=%async_computation.1 | async-start | bytes 9437184 | tf_op jit(solution)/shard_map/all_gather | solution.py:15
  7.3 265.3 %all-gather.6.cloned.1.call-start = ((), (), s32[]{:S(2)}) async-start(), calls=%async_computation.2 | async-start | bytes 9437184 | tf_op jit(solution)/shard_map/all_gather | solution.py:22
  8.0 440.6 %all-gather.8.cloned.1.call-start = ((), (), s32[]{:S(2)}) async-start(), calls=%async_computation.3 | async-start | bytes 20971520 | tf_op jit(solution)/shard_map/all_gather | solution.py:38
  292.7 0.7 copy-start
  292.7 4.3 copy-start.1
Sparse Core Ops, SparseCore 0:
  8.9 84.7 all-gather.3
  95.3 151.0 all-gather.5
  292.9 155.6 all-gather.7
where the time goes:
time: 478 us; the launch traced here: 477 us
  waiting for transfers between devices  238 us (50%)
  blocking collectives  149 us (31%)
  matrix products  49 us (10%)
  local copies, waits for them, and re-layouts  28 us (6%)
  between operations  13.1 us (3%)
    all_gather x1, waiting for transfers between devices, shards(): lax.all_gather(rotated, 'pair', axis=0, tiled=True)  151 us
    all_to_all x1, blocking collectives, shards(): lax.all_to_all(half_rot, 'mat', split_axis=2, concat_axis=1, tiled=True)  149 us
    all_gather x1, waiting for transfers between devices, shards(): lax.all_gather(right_rot, 'mat', axis=0, tiled=True)  85.7 us
    dot_general x1, matrix products, shards(): jnp.einsum('tk,kmc->tmc', coupling, lax.all_gather(rotated, 'pair', axis=...  17.5 us
    dot_general x1, matrix products, shards(): jnp.einsum('rm,krc->kmc', lax.all_gather(left_rot, 'mat', axis=0, tiled=T...  13.9 us
    dot_general x1, matrix products, shards(): jnp.einsum('krj,jm->krm', operators, lax.all_gather(right_rot, 'mat', axi...  13.8 us
  transfers between devices with their start and end apart: 3, of which 2 were waited for; matrix products, arithmetic and copies ran while one was open for 7% of the time, Pallas kernels for 0%

commit v1 on v0

v1 whole, which is shorter than its diff:
```python
import jax
import jax.numpy as jnp
from jax import lax
from jax.sharding import PartitionSpec as P


def selector(indices, count):
    return (indices[:, None] == jnp.arange(count, dtype=jnp.int32)[None, :]).astype(jnp.float32)


def shards(operators, left_rot, right_rot, integrals, pair_index, target_index):
    npairs = integrals.shape[0]
    rowsel = jnp.dot(selector(target_index, npairs), integrals, precision=lax.Precision.HIGHEST)
    coupling = jnp.dot(
        rowsel, selector(pair_index, npairs).T, precision=lax.Precision.HIGHEST
    ).astype(jnp.bfloat16)
    right = lax.all_gather(right_rot, "mat", axis=0, tiled=True)
    left = lax.all_gather(left_rot, "mat", axis=0, tiled=True)
    strips = lax.all_to_all(operators, "pair", split_axis=1, concat_axis=0, tiled=True)
    mixed = jnp.einsum(
        "tk,krj->trj", coupling, strips, preferred_element_type=jnp.float32
    ).astype(jnp.bfloat16)
    half = jnp.einsum(
        "trj,jm->trm", mixed, right, preferred_element_type=jnp.float32
    ).astype(jnp.bfloat16)
    ntgt, rows, cols = half.shape
    npair = lax.axis_size("pair")
    nmat = lax.axis_size("mat")
    blocks = half.reshape(npair, ntgt // npair, rows, nmat, cols // nmat)
    blocks = blocks.transpose(0, 3, 1, 2, 4)
    blocks = blocks.reshape((npair * nmat,) + blocks.shape[2:])
    got = lax.all_to_all(blocks, ("pair", "mat"), split_axis=0, concat_axis=0, tiled=True)
    got = got.reshape((npair, nmat) + got.shape[1:])
    columns = got.transpose(2, 1, 0, 3, 4).reshape(ntgt // npair, cols, cols // nmat)
    return jnp.einsum(
        "rm,trc->tmc", left, columns, preferred_element_type=jnp.float32
    ).astype(jnp.bfloat16)


def solution(mesh):
    in_specs = (P("pair", "mat", None), P("mat", None), P("mat", None), P(), P(), P())
    out_specs = P("pair", None, "mat")
    return jax.shard_map(shards, mesh=mesh, in_specs=in_specs, out_specs=out_specs, check_vma=False)
```

time: 478 us -> 295 us (0.62)
  waiting for transfers between devices: 238 us -> 58.3 us
  matrix products: 49 us -> 38.9 us
  blocking collectives: 149 us -> 155 us
  starting transfers between devices: 0.08 us -> 5.36 us
    all_gather x3 -> x2, waiting for transfers between devices: 237 us -> 12.2 us  [the longest x1 12.2 us: shards(): right = lax.all_gather(right_rot, 'mat', axis=0, tiled=True)]
    all_to_all x0 -> x1, waiting for transfers between devices: none -> 44.7 us  [shards(): lax.all_to_all(operators, 'pair', split_axis=1, concat_axis=0, tiled=True)]
    convert_element_type x3 -> x1, local copies, waits for them, and re-layouts: 18.5 us -> 6.18 us  [shards(): return jnp.einsum('rm,trc->tmc', left, columns, preferred_element_type=jn...]
    dot_general x4, matrix products: 48.8 us -> 38.7 us  [the longest x1 14 us: shards(): jnp.einsum('rm,trc->tmc', left, columns, preferred_element_type=jnp.float32)]
    unnamed x4 -> x6, local copies, waits for them, and re-layouts: 0.63 us -> 8.93 us
    all_to_all x1, blocking collectives: 149 us -> 155 us  [shards(): lax.all_to_all(blocks, ('pair', 'mat'), split_axis=0, concat_axis=0, tile...]
    all_to_all x0 -> x1, starting transfers between devices: none -> 5.32 us  [shards(): lax.all_to_all(operators, 'pair', split_axis=1, concat_axis=0, tiled=True)]
  transfers between devices with their start and end apart: 3 -> 3, of which waited for: 2 -> 2; matrix products, arithmetic and copies ran while one was open for 7% -> 14% of each run, Pallas kernels for 0% -> 0%
where the time goes in v1:
time: 295 us
  blocking collectives  155 us (53%)
  waiting for transfers between devices  58.3 us (20%)
  matrix products  38.9 us (13%)
  local copies, waits for them, and re-layouts  23.6 us (8%)
  between operations  13.4 us (5%)
  starting transfers between devices  5.36 us (2%)
    all_to_all x1, blocking collectives, shards(): lax.all_to_all(blocks, ('pair', 'mat'), split_axis=0, concat_axis=0, tile...  155 us
    all_to_all x1, waiting for transfers between devices, shards(): lax.all_to_all(operators, 'pair', split_axis=1, concat_axis=0, tiled=True)  44.7 us
    dot_general x1, matrix products, shards(): jnp.einsum('rm,trc->tmc', left, columns, preferred_element_type=jnp.float32)  14 us
    dot_general x1, matrix products, shards(): jnp.einsum('trj,jm->trm', mixed, right, preferred_element_type=jnp.float32)  14 us
    all_gather x1, waiting for transfers between devices, shards(): right = lax.all_gather(right_rot, 'mat', axis=0, tiled=True)  12.2 us
    unnamed x6, local copies, waits for them, and re-layouts  8.93 us
    dot_general x1, matrix products, shards(): jnp.einsum('tk,krj->trj', coupling, strips, preferred_element_type=jnp.fl...  6.76 us
    convert_element_type x1, local copies, waits for them, and re-layouts, shards(): return jnp.einsum('rm,trc->tmc', left, columns, preferred_element_type=jn...  6.18 us
  transfers between devices with their start and end apart: 3, of which 2 were waited for; matrix products, arithmetic and copies ran while one was open for 14% of the time, Pallas kernels for 0%

profile of v1, /device:TPU:0, one launch (start us, length us, event | category | flops | bytes accessed | tf_op | source)
XLA Modules:
  0.0 294.7 jit_solution(3088542971423130391)
XLA Ops:
  6.5 0.0 all-gather.3.cloned.1.call-start
  6.5 0.7 all-gather.3.cloned.1.call-update
  7.3 0.0 all-gather.5.cloned.1.call-start
  7.3 0.7 all-gather.5.cloned.1.call-update
  8.0 7.4 %copy.19 = bf16[4,256,2048]{2,0,1:T(4,128)(2,1)} copy(bf16[4,256,2048]{2,1,0:T(8,128)(2,1)} %param.6) | data formatting | bytes 8388608 | tf_op args[0]
  15.4 0.0 copy-start
  15.4 5.3 %all-to-all-start = ((bf16[4,256,2048]{2,0,1:T(4,128)(2,1)}), bf16[4,256,2048]{2,0,1:T(4,128)(2,1)}, u32[]{:S(2)}, u32[]{:S(2)}) async-start(bf16[4,256,2048]{2,0,1:T(4,128)(2,1)} %copy.19), calls=%async_computation | async-start | bytes 8388608 | tf_op jit(solution)/shard_map/all_to_all | solution.py:19
  20.8 0.0 copy-done
  20.8 0.0 copy-start.1
  20.8 4.0 %fusion.18 = f32[16,1024]{1,0:T(8,128)S(1)} fusion(f32[1024,1024]{1,0:T(8,128)} %param.9, s32[16]{0:T(128)S(1)} %copy-done), kind=kOutput, calls=%fused_computation.14 | convolution fusion | flops 201342976 | bytes 4259904 | tf_op jit(solution)/shard_map/dot_general | solution.py:13
  24.7 0.0 copy-done.1
  24.7 0.2 fusion.17
  24.9 44.7 %all-to-all-done = bf16[4,256,2048]{2,0,1:T(4,128)(2,1)} async-done(((bf16[4,256,2048]{2,0,1:T(4,128)(2,1)}), bf16[4,256,2048]{2,0,1:T(4,128)(2,1)}, u32[]{:S(2)}, u32[]{:S(2)}) %all-to-all-start) | async-done | bytes 4194336 | tf_op jit(solution)/shard_map/all_to_all | solution.py:19
  69.7 4.5 %copy.20 = bf16[4,256,2048]{2,1,0:T(8,128)(2,1)S(1)} copy(bf16[4,256,2048]{2,0,1:T(4,128)(2,1)} %all-to-all-done) | data formatting | bytes 8388608 | tf_op jit(solution)/shard_map/all_to_all | solution.py:19
  74.2 0.6 copy.21
  74.8 6.8 %fusion.7 = bf16[16,64,2048]{2,0,1:T(8,128)(2,1)} fusion(bf16[16,16,1]{1,0,2:T(8,128)(2,1)S(1)} %fusion.17, bf16[16,64,2048]{2,1,0:T(8,128)(2,1)S(1)} %bitcast.37), kind=kOutput, calls=%fused_computation.8 | convolution fusion | flops 69206016 | bytes 8389120 | tf_op jit(solution)/shard_map/tk,krj->trj/dot_general | solution.py:20
  81.6 12.2 %all-gather.3.cloned.1.call-done = bf16[2048,2048]{1,0:T(8,128)(2,1)} async-done(((bf16[256,2048]{1,0:T(8,128)(2,1)}), bf16[2048,2048]{1,0:T(8,128)(2,1)}) %all-gather.3.cloned.1.call-update) | async-done | bytes 8388624 | tf_op jit(solution)/shard_map/all_gather | solution.py:17
  93.7 14.0 %fusion.10 = bf16[16,64,2048]{2,1,0:T(8,128)(2,1)S(1)} fusion(bf16[2048,2048]{1,0:T(8,128)(2,1)} %all-gather.3.cloned.1.call-done, bf16[16,64,2048]{2,0,1:T(8,128)(2,1)} %fusion.7), kind=kOutput, calls=%fused_computation.9 | convolution fusion | flops 8592031744 | bytes 16777216 | tf_op jit(solution)/shard_map/trj,jm->trm/dot_general | solution.py:23
  107.7 1.5 copy.29
  109.2 1.0 copy.24
  110.2 155.2 %all_to_all.23 = bf16[32,4,64,256]{3,2,1,0:T(8,128)(2,1)S(1)} all-to-all(bf16[32,4,64,256]{3,2,1,0:T(8,128)(2,1)S(1)} %bitcast.35), channel_id=1, replica_groups=mesh['pair'=4,'mat'=8] {'pair','mat'}, dimensions={0} | all-to-all | bytes 8388608 | tf_op jit(solution)/shard_map/all_to_all | solution.py:32
  265.4 2.3 copy.25
  267.7 0.0 all-gather.5.cloned.1.call-done
  267.7 14.0 %convert_bitcast_fusion = bf16[4,2048,256]{1,2,0:T(8,128)(2,1)} fusion(bf16[4,2048,256]{2,1,0:T(8,128)(2,1)} %bitcast.38, bf16[2048,2048]{1,0:T(8,128)(2,1)} %all-gather.5.cloned.1.call-done), kind=kOutput, calls=%fused_computation.7 | convolution fusion | flops 8592031744 | bytes 16777216 | tf_op jit(solution)/shard_map/rm,trc->tmc/dot_general | solution.py:35
  281.7 6.2 %copy.27 = bf16[4,2048,256]{2,1,0:T(8,128)(2,1)} copy(bf16[4,2048,256]{1,2,0:T(8,128)(2,1)} %convert_bitcast_fusion) | data formatting | bytes 8388608 | tf_op jit(solution)/shard_map/convert_element_type | solution.py:37
Async XLA Ops:
  6.5 87.2 %all-gather.3.cloned.1.call-start = ((), (), s32[]{:S(2)}) async-start(), calls=%async_computation.2 | async-start | bytes 9437184 | tf_op jit(solution)/shard_map/all_gather | solution.py:17
  7.3 260.5 %all-gather.5.cloned.1.call-start = ((), (), s32[]{:S(2)}) async-start(), calls=%async_computation.3 | async-start | bytes 9437184 | tf_op jit(solution)/shard_map/all_gather | solution.py:18
  15.4 5.3 %copy-start = (s32[16]{0:T(128)S(1)}, s32[16]{0:T(128)}, u32[]{:S(2)}) copy-start(s32[16]{0:T(128)} %param.11) | copy-start | bytes 196
  15.4 54.2 %all-to-all-start = ((bf16[4,256,2048]{2,0,1:T(4,128)(2,1)}), bf16[4,256,2048]{2,0,1:T(4,128)(2,1)}, u32[]{:S(2)}, u32[]{:S(2)}) async-start(bf16[4,256,2048]{2,0,1:T(4,128)(2,1)} %copy.19), calls=%async_computation | async-start | bytes 8388608 | tf_op jit(solution)/shard_map/all_to_all | solution.py:19
  20.8 4.0 %copy-start.1 = (s32[16]{0:T(128)S(1)}, s32[16]{0:T(128)}, u32[]{:S(2)}) copy-start(s32[16]{0:T(128)} %param.10) | copy-start | bytes 196
Sparse Core Ops, SparseCore 0:
  8.9 84.7 all-gather.2
  95.3 154.0 all-gather.4

commit v2 on v1

v2 whole, which is shorter than its diff:
```python
import jax
import jax.numpy as jnp
from jax import lax
from jax.sharding import Mesh, PartitionSpec as P


CORES = 2
MAT = ("line", "core")


def selector(indices, count):
    return (indices[:, None] == jnp.arange(count, dtype=jnp.int32)[None, :]).astype(jnp.float32)


def own_piece(mine):
    piece = mine.shape[0] // lax.axis_size("pair")
    return lax.dynamic_slice_in_dim(mine, lax.axis_index("pair") * piece, piece, 0)


def in_plane(along):
    whole = lax.all_gather(along, ("core", "pair"), axis=1)
    return whole.reshape(-1, along.shape[-1])


def shards(operators, left_rot, right_rot, integrals, pair_index, target_index):
    npairs = integrals.shape[0]
    npair = lax.axis_size("pair")
    nmat = lax.axis_size("line") * lax.axis_size("core")
    own, rows, cols = operators.shape
    piece = rows // npair
    width = cols // nmat

    right_a = right_rot
    outgoing = operators.reshape(own, npair, piece, cols).transpose(1, 0, 2, 3)
    outgoing = outgoing.reshape(npair, own * piece, cols)
    strips = lax.all_to_all(outgoing, "pair", split_axis=0, concat_axis=0, tiled=True)
    whole_a = lax.all_gather(right_a, MAT, axis=0, tiled=True)
    along_l = lax.all_gather(own_piece(left_rot), "line", axis=0)
    left = in_plane(along_l)

    rowsel = jnp.dot(selector(target_index, npairs), integrals, precision=lax.Precision.HIGHEST)
    coupling = jnp.dot(rowsel, selector(pair_index, npairs).T, precision=lax.Precision.HIGHEST).astype(jnp.bfloat16)
    strips = strips.reshape(own * npair, piece, cols)
    mixed = jnp.einsum(
        "tk,krj->trj", coupling, strips, preferred_element_type=jnp.float32
    ).astype(jnp.bfloat16)
    ntgt = mixed.shape[0]

    def half_swap(right):
        half = jnp.einsum(
            "trj,jm->trm", mixed, right, preferred_element_type=jnp.float32
        ).astype(jnp.bfloat16)
        blocks = half.reshape(npair, ntgt // npair, piece, nmat, width)
        blocks = blocks.transpose(0, 3, 1, 2, 4)
        blocks = blocks.reshape(npair * nmat, ntgt // npair * piece, width)
        return lax.all_to_all(blocks, ("pair",) + MAT, split_axis=0, concat_axis=0, tiled=True)

    def finish(got):
        got = got.reshape(npair, nmat, ntgt // npair, piece, width)
        columns = got.transpose(2, 1, 0, 3, 4).reshape(ntgt // npair, cols, width)
        return jnp.einsum(
            "rm,trc->tmc", left, columns, preferred_element_type=jnp.float32
        ).astype(jnp.bfloat16)

    got_a = half_swap(whole_a)
    return finish(got_a)


def solution(mesh):
    npair, nmat = mesh.shape["pair"], mesh.shape["mat"]
    fine = Mesh(mesh.devices.reshape(npair, nmat // CORES, CORES), ("pair",) + MAT)
    in_specs = (P("pair", MAT, None), P(MAT, None), P(MAT, None), P(), P(), P())
    out_specs = P("pair", None, MAT)
    return jax.shard_map(shards, mesh=fine, in_specs=in_specs, out_specs=out_specs, check_vma=False)
```

time: 295 us -> 267 us (0.905)
  blocking collectives: 155 us -> 97.8 us
  waiting for transfers between devices: 58.3 us -> 90.9 us
  local copies, waits for them, and re-layouts: 23.6 us -> 17.7 us
    all_to_all x1, blocking collectives: 155 us -> 97.8 us  [half_swap(): lax.all_to_all(blocks, ('pair',) + MAT, split_axis=0, concat_axis=0, tile...]
    all_gather x2 -> x3, waiting for transfers between devices: 12.2 us -> 47.4 us  [the longest x1 30.3 us: shards(): along_l = lax.all_gather(own_piece(left_rot), 'line', axis=0)]
    unnamed x6 -> x9, local copies, waits for them, and re-layouts: 8.93 us -> 2.72 us
    all_to_all x2 -> x0, local copies, waits for them, and re-layouts: 5.12 us -> none  [shards(): lax.all_to_all(operators, 'pair', split_axis=1, concat_axis=0, tiled=True)]
    transpose x1 -> x2, local copies, waits for them, and re-layouts: 2.32 us -> 7.11 us  [the longest x1 4.79 us: shards(): outgoing = operators.reshape(own, npair, piece, cols).transpose(1, 0, 2, 3)]
  transfers between devices with their start and end apart: 3 -> 4, of which waited for: 2 -> 3; matrix products, arithmetic and copies ran while one was open for 14% -> 14% of each run, Pallas kernels for 0% -> 0%
where the time goes in v2:
time: 267 us; the launch traced here: 266 us
  blocking collectives  97.8 us (37%)
  waiting for transfers between devices  90.9 us (34%)
  matrix products  41.5 us (16%)
  local copies, waits for them, and re-layouts  17.7 us (7%)
  between operations  13.2 us (5%)
  starting transfers between devices  5.16 us (2%)
    all_to_all x1, blocking collectives, half_swap(): lax.all_to_all(blocks, ('pair',) + MAT, split_axis=0, concat_axis=0, tile...  97.8 us
    all_to_all x1, waiting for transfers between devices, shards(): lax.all_to_all(outgoing, 'pair', split_axis=0, concat_axis=0, tiled=True)  42.8 us
    all_gather x1, waiting for transfers between devices, shards(): along_l = lax.all_gather(own_piece(left_rot), 'line', axis=0)  30.3 us
    all_gather x1, waiting for transfers between devices, shards(): whole_a = lax.all_gather(right_a, MAT, axis=0, tiled=True)  17.1 us
    dot_general x1, matrix products, half_swap(): jnp.einsum('trj,jm->trm', mixed, right, preferred_element_type=jnp.float32)  14.1 us
    dot_general x1, matrix products, finish(): jnp.einsum('rm,trc->tmc', left, columns, preferred_element_type=jnp.float32)  14.1 us
    dot_general x1, matrix products, shards(): jnp.einsum('tk,krj->trj', coupling, strips, preferred_element_type=jnp.fl...  8.94 us
    convert_element_type x1, local copies, waits for them, and re-layouts, finish(): return jnp.einsum('rm,trc->tmc', left, columns, preferred_element_type=jn...  6.18 us
  transfers between devices with their start and end apart: 4, of which 3 were waited for; matrix products, arithmetic and copies ran while one was open for 14% of the time, Pallas kernels for 0%

profile of v2, /device:TPU:0, one launch (start us, length us, event | category | flops | bytes accessed | tf_op | source)
XLA Modules:
  0.0 266.2 jit_solution(47326333321936205)
XLA Ops:
  6.5 0.0 copy-start
  6.5 0.0 all-gather.8.cloned.1.call-start
  6.5 1.2 copy-done
  7.8 0.7 constant_dynamic-slice_fusion
  8.5 0.0 all-gather.8.cloned.1.call-update
  8.5 0.0 all-gather.6.cloned.1.call-start
  8.6 0.7 all-gather.6.cloned.1.call-update
  9.3 0.0 all-gather.10.cloned.1.call-start
  9.3 30.3 %all-gather.8.cloned.1.call-done = bf16[256,2048]{1,0:T(8,128)(2,1)} async-done(((bf16[64,2048]{1,0:T(8,128)(2,1)}), bf16[256,2048]{1,0:T(8,128)(2,1)}) %all-gather.8.cloned.1.call-update) | async-done | bytes 1048592 | tf_op jit(solution)/shard_map/all_gather | solution.py:38
  39.6 0.0 all-gather.10.cloned.1.call-update
  39.7 4.8 %copy.18 = bf16[4,4,64,2048]{3,2,1,0:T(8,128)(2,1)} copy(bf16[4,4,64,2048]{3,2,0,1:T(8,128)(2,1)} %bitcast.38) | data formatting | bytes 8388608 | tf_op jit(solution)/shard_map/transpose | solution.py:34
  44.5 0.0 copy-start.2
  44.5 5.1 %all-to-all-start = ((bf16[4,256,2048]{2,1,0:T(8,128)(2,1)}), bf16[4,256,2048]{2,1,0:T(8,128)(2,1)}, u32[]{:S(2)}, u32[]{:S(2)}) async-start(bf16[4,256,2048]{2,1,0:T(8,128)(2,1)} %bitcast.34), calls=%async_computation | async-start | bytes 8388608 | tf_op jit(solution)/shard_map/all_to_all | solution.py:36
  49.5 0.0 copy-done.2
  49.6 0.0 copy-start.3
  49.6 4.1 %fusion.14 = f32[16,1024]{1,0:T(8,128)S(1)} fusion(f32[1024,1024]{1,0:T(8,128)} %param.9, s32[16]{0:T(128)S(1)} %copy-done.2), kind=kOutput, calls=%fused_computation.12 | convolution fusion | flops 201342976 | bytes 4259904 | tf_op jit(solution)/shard_map/dot_general | solution.py:41
  53.7 0.0 copy-done.3
  53.7 0.2 fusion.13
  53.9 42.8 %all-to-all-done = bf16[4,256,2048]{2,1,0:T(8,128)(2,1)} async-done(((bf16[4,256,2048]{2,1,0:T(8,128)(2,1)}), bf16[4,256,2048]{2,1,0:T(8,128)(2,1)}, u32[]{:S(2)}, u32[]{:S(2)}) %all-to-all-start) | async-done | bytes 4194336 | tf_op jit(solution)/shard_map/all_to_all | solution.py:36
  96.7 8.9 %fusion.5 = bf16[16,64,2048]{2,0,1:T(8,128)(2,1)} fusion(bf16[16,16,1]{1,0,2:T(8,128)(2,1)S(1)} %fusion.13, bf16[16,64,2048]{2,1,0:T(8,128)(2,1)} %bitcast.4), kind=kOutput, calls=%fused_computation.6 | convolution fusion | flops 69206016 | bytes 8389120 | tf_op jit(solution)/shard_map/tk,krj->trj/dot_general | solution.py:44
  105.6 17.1 %all-gather.6.cloned.1.call-done = bf16[2048,2048]{1,0:T(8,128)(2,1)} async-done(((bf16[256,2048]{1,0:T(8,128)(2,1)}), bf16[2048,2048]{1,0:T(8,128)(2,1)}) %all-gather.6.cloned.1.call-update) | async-done | bytes 8388624 | tf_op jit(solution)/shard_map/all_gather | solution.py:37
  122.7 14.1 %fusion.8 = bf16[16,64,2048]{2,1,0:T(8,128)(2,1)S(1)} fusion(bf16[2048,2048]{1,0:T(8,128)(2,1)} %all-gather.6.cloned.1.call-done, bf16[16,64,2048]{2,0,1:T(8,128)(2,1)} %fusion.5), kind=kOutput, calls=%fused_computation.7 | convolution fusion | flops 8592031744 | bytes 16777216 | tf_op jit(solution)/shard_map/trj,jm->trm/dot_general | solution.py:50
  136.8 1.5 copy.26
  138.3 1.0 copy.21
  139.3 97.8 %all_to_all.10 = bf16[32,256,256]{2,1,0:T(8,128)(2,1)S(1)} all-to-all(bf16[32,256,256]{2,1,0:T(8,128)(2,1)S(1)} %bitcast.36), channel_id=1, replica_groups=mesh['pair'=4,'line'=4,'core'=2] {'pair','line','core'}, dimensions={0} | all-to-all | bytes 8388608 | tf_op jit(solution)/shard_map/all_to_all | solution.py:56
  237.1 2.3 copy.22
  239.4 0.0 all-gather.10.cloned.1.call-done
  239.5 0.0 copy-start.1
  239.5 14.1 %convert_bitcast_fusion = bf16[4,2048,256]{1,2,0:T(8,128)(2,1)} fusion(bf16[4,2048,256]{2,1,0:T(8,128)(2,1)} %bitcast.39, bf16[2048,2048,1]{1,0,2:T(8,128)(2,1)} %bitcast.42), kind=kOutput, calls=%fused_computation.5 | convolution fusion | flops 8592031744 | bytes 16777216 | tf_op jit(solution)/shard_map/rm,trc->tmc/dot_general | solution.py:61
  253.5 6.2 %copy.24 = bf16[4,2048,256]{2,1,0:T(8,128)(2,1)} copy(bf16[4,2048,256]{1,2,0:T(8,128)(2,1)} %convert_bitcast_fusion) | data formatting | bytes 8388608 | tf_op jit(solution)/shard_map/convert_element_type | solution.py:63
  259.7 0.0 copy-done.1
Async XLA Ops:
  6.5 1.2 copy-start
  6.5 33.1 %all-gather.8.cloned.1.call-start = ((), (), s32[]{:S(2)}) async-start(), calls=%async_computation.3 | async-start | bytes 1310720 | tf_op jit(solution)/shard_map/all_gather | solution.py:38
  8.5 114.2 %all-gather.6.cloned.1.call-start = ((), (), s32[]{:S(2)}) async-start(), calls=%async_computation.2 | async-start | bytes 9437184 | tf_op jit(solution)/shard_map/all_gather | solution.py:37
  9.3 230.2 %all-gather.10.cloned.1.call-start = ((), (), s32[]{:S(2)}) async-start(), calls=%async_computation.4 | async-start | bytes 9437184 | tf_op jit(solution)/shard_map/all_gather | solution.py:21
  44.5 5.1 %copy-start.2 = (s32[16]{0:T(128)S(1)}, s32[16]{0:T(128)}, u32[]{:S(2)}) copy-start(s32[16]{0:T(128)} %param.11) | copy-start | bytes 196
  44.5 52.2 %all-to-all-start = ((bf16[4,256,2048]{2,1,0:T(8,128)(2,1)}), bf16[4,256,2048]{2,1,0:T(8,128)(2,1)}, u32[]{:S(2)}, u32[]{:S(2)}) async-start(bf16[4,256,2048]{2,1,0:T(8,128)(2,1)} %bitcast.34), calls=%async_computation | async-start | bytes 8388608 | tf_op jit(solution)/shard_map/all_to_all | solution.py:36
  49.6 4.1 %copy-start.3 = (s32[16]{0:T(128)S(1)}, s32[16]{0:T(128)}, u32[]{:S(2)}) copy-start(s32[16]{0:T(128)} %param.10) | copy-start | bytes 196
  239.5 20.3 %copy-start.1 = (bf16[256,2048]{1,0:T(8,128)(2,1)S(1)}, bf16[256,2048]{1,0:T(8,128)(2,1)}, u32[]{:S(2)}) copy-start(bf16[256,2048]{1,0:T(8,128)(2,1)} %param.7) | copy-start | bytes 3145732
Sparse Core Ops, SparseCore 0:
  8.9 30.6 all-gather.7
  41.2 81.3 all-gather.5
  124.6 81.6 all-gather.9
